TPU v7x, 32 devices: a whole 2x2x4 slice. The times are simulated.
32 devices in a mesh: region: 4 (over y, core), member: 8 (over z, x).
Axes of the slice: x: 2, y: 2, z: 4, core: 2. Of those that a mesh axis runs over, the one named last changes fastest.
Arguments:
- initial_ensemble: float32 [256, 32768], P('member', 'region'), may hold values from -18 to 18
- driving_term: float32 [32768], P('region'), may hold values from 4 to 12
- observation_cells: int32 [1, 2, 64, 128], P(None, None, ('region', 'member')), may hold values from 0 to 1023
- observation_values: float32 [1, 2, 64, 128], P(None, None, ('region', 'member')), may hold values from -12 to 12
- observation_weight: float32 [1, 2, 64, 128], P(None, None, ('region', 'member')), may hold values from 0.25 to 4
- block_tile_list: int32 [1, 2, 64, 4], P(None, None, ('region', 'member')), may hold values from 0 to 63, as said below
- block_tile_count: int32 [1, 2, 64], P(None, None, ('region', 'member')), may hold values from 1 to 4, as said below
Outputs:
- analysis: float32 [256, 32768], P('member', 'region')
Inputs may be any that keep to these rules, and one draw needn't show every extreme that they name: For s < block_tile_count[c, p, b] the entries block_tile_list[c, p, b, s] are distinct tiles whose owner t // 2 is b // 2 - 1, b // 2 or b // 2 + 1, taken modulo 64 // 2; entries at s >= block_tile_count[c, p, b] are ignored. `block_tile_count`: in every cycle and pass some block lists 4 tiles.
All inputs are finite; a program needn't handle non-finite values.
Results may differ from a plain program's by a relative error of at most 0.0003.
Values sent between devices are 32-bit elements; how exact they have to be, the bound alone decides.
A program may use at most 64 MiB of HBM per device.

v0:
```python
import functools
import math

import jax
import jax.numpy as jnp
from jax import lax
from jax.experimental import pallas as pl
from jax.experimental.pallas import tpu as pltpu
from jax.sharding import PartitionSpec as P

BLOCK = 512
NS_ITERS = 10
STEPS = 4
PASSES = 2
BEHIND = 2 * STEPS
AHEAD = STEPS

time_step = 0.05


def with_halo(cells, sides, width):
    for axis, dim in sides:
        count = lax.axis_size(axis)
        head = lax.slice_in_dim(cells, 0, width, axis=dim)
        tail = lax.slice_in_dim(cells, cells.shape[dim] - width, cells.shape[dim], axis=dim)
        cells = jnp.concatenate(
            [
                lax.ppermute(tail, axis, [(i, (i + 1) % count) for i in range(count)]),
                cells,
                lax.ppermute(head, axis, [((i + 1) % count, i) for i in range(count)]),
            ],
            axis=dim,
        )
    return cells


def forward_ring(count):
    return [(i, (i + 1) % count) for i in range(count)]


def backward_ring(count):
    return [((i + 1) % count, i) for i in range(count)]


def forecast(ensemble, driving_term):
    count = lax.axis_size("region")
    width = ensemble.shape[1]
    edge = jnp.concatenate(
        [ensemble, jnp.broadcast_to(driving_term[None], (8, width))], axis=0
    )
    behind = lax.ppermute(edge[:, width - BEHIND :], "region", forward_ring(count))
    ahead = lax.ppermute(edge[:, :AHEAD], "region", backward_ring(count))
    members = ensemble.shape[0]
    wide = jnp.concatenate([behind[:members], ensemble, ahead[:members]], axis=1)
    forcing = jnp.concatenate([behind[members], driving_term, ahead[members]])
    for _ in range(STEPS):
        inner = wide.shape[1] - 3
        wide = wide[:, 2 : inner + 2] + time_step * (
            (wide[:, 3:] - wide[:, :inner]) * wide[:, 1 : inner + 1]
            - wide[:, 2 : inner + 2]
            + forcing[2 : inner + 2]
        )
        forcing = forcing[2 : inner + 2]
    return wide


def split(value):
    high = value.astype(jnp.bfloat16)
    low = (value - high.astype(jnp.float32)).astype(jnp.bfloat16)
    return high, low


def dot3(left, right, contract=((1,), (0,))):
    def one(a, b):
        return lax.dot_general(
            a, b, (contract, ((), ())), preferred_element_type=jnp.float32
        )

    return one(left[0], right[0]) + (one(left[0], right[1]) + one(left[1], right[0]))


def roots(systems, identity):
    frobs = [jnp.sqrt(jnp.sum(s * s, keepdims=True)) for s in systems]
    firsts = [s / f for s, f in zip(systems, frobs)]

    def quartic(error):
        halves = split(error)
        square = dot3(halves, halves)
        rest = 0.375 * identity + 0.3125 * error + 0.0625 * square
        return 0.5 * error + dot3(split(square), split(rest))

    def close(inv, root):
        return identity - dot3(split(inv), split(root))

    invs, rts, errors = [], [], []
    for first in firsts:
        q = quartic(identity - first)
        invs.append(identity + q)
        rts.append(first + dot3(split(first), split(q)))
    errors = [close(i, r) for i, r in zip(invs, rts)]
    count = len(systems)

    def step(_, state):
        invs, rts, errors = state
        qs = [split(quartic(e)) for e in errors]
        invs = [i + dot3(split(i), q) for i, q in zip(invs, qs)]
        rts = [r + dot3(split(r), q) for r, q in zip(rts, qs)]
        return invs, rts, [close(i, r) for i, r in zip(invs, rts)]

    invs, rts, errors = lax.fori_loop(0, NS_ITERS // 2 - 2, step, (invs, rts, errors))
    qs = [split(quartic(e)) for e in errors]
    invs = [i + dot3(split(i), q) for i, q in zip(invs, qs)]
    return [i / jnp.sqrt(f) for i, f in zip(invs, frobs)]


def analysis_kernel(member_ref, tiles_ref, ens_ref, out_ref):
    blocks, tiles = member_ref.shape
    members = ens_ref.shape[0]
    rows = lax.broadcasted_iota(jnp.int32, (members, members), 0)
    columns = lax.broadcasted_iota(jnp.int32, (members, members), 1)
    identity = (rows == columns).astype(jnp.float32)
    grams = [(members - 1.0) * identity for _ in range(blocks)]
    pulls = [jnp.zeros((members, 1), jnp.float32) for _ in range(blocks)]
    for t in range(tiles):
        spread = tiles_ref[t, :members, :]
        innovation = tiles_ref[t, members : members + 1, :]
        halves = split(spread)
        gram = dot3(halves, halves, ((1,), (1,)))
        pull = jnp.sum(spread * innovation, axis=1, keepdims=True)
        for b in range(blocks):
            weight = member_ref[b, t]
            grams[b] = grams[b] + weight * gram
            pulls[b] = pulls[b] + weight * pull
    inv_roots = roots(grams, identity)
    for b in range(blocks):
        inv_root = inv_roots[b]
        inner = jnp.sum(inv_root * pulls[b], axis=0, keepdims=True)
        shift = jnp.sum(inv_root * inner, axis=1, keepdims=True)
        cells = ens_ref[:, b * BLOCK : (b + 1) * BLOCK]
        center = jnp.mean(cells, axis=0, keepdims=True)
        anomaly = cells - center
        base = center + jnp.sum(shift * anomaly, axis=0, keepdims=True)
        scaled = split(math.sqrt(members - 1) * inv_root)
        out_ref[:, b * BLOCK : (b + 1) * BLOCK] = base + dot3(scaled, split(anomaly))


def analyse(member_ship, nearby, ensemble):
    return pl.pallas_call(
        analysis_kernel,
        out_shape=jax.ShapeDtypeStruct(ensemble.shape, jnp.float32),
        in_specs=[
            pl.BlockSpec(memory_space=pltpu.SMEM),
            pl.BlockSpec(memory_space=pltpu.VMEM),
            pl.BlockSpec(memory_space=pltpu.VMEM),
        ],
        out_specs=pl.BlockSpec(memory_space=pltpu.VMEM),
    )(member_ship, nearby, ensemble)


def tile_pack(ensemble, cell_index, values, weight):
    picked = ensemble[:, cell_index]
    center = jnp.mean(picked, axis=0)
    root_weight = jnp.sqrt(weight)
    spread = (picked - center) * root_weight
    innovation = (values - center) * root_weight
    return jnp.concatenate([jnp.transpose(spread, (1, 0, 2)), innovation[:, None, :]], axis=1)


def memberships(listed, counts, device, devices, tiles_here):
    slot_ids = (listed - (device - 1) * tiles_here) % (devices * tiles_here)
    living = lax.broadcasted_iota(jnp.int32, listed.shape, 2) < counts[:, :, None]
    candidates = lax.broadcasted_iota(jnp.int32, (1, 1, 1, 3 * tiles_here), 3)
    chosen = living[..., None] & (slot_ids[..., None] == candidates)
    return jnp.sum(chosen.astype(jnp.float32), axis=2)


def local(
    initial_ensemble,
    driving_term,
    observation_cells,
    observation_values,
    observation_weight,
    block_tile_list,
    block_tile_count,
):
    device = lax.axis_index("region") * lax.axis_size("member") + lax.axis_index("member")
    devices = lax.axis_size("region") * lax.axis_size("member")
    tiles_here = observation_cells.shape[2]
    member_ship = memberships(block_tile_list[0], block_tile_count[0], device, devices, tiles_here)
    replica = forecast(initial_ensemble, driving_term)
    ensemble = lax.all_to_all(replica, "member", split_axis=1, concat_axis=0, tiled=True)
    for p in range(PASSES):
        packed = tile_pack(
            ensemble, observation_cells[0, p], observation_values[0, p], observation_weight[0, p]
        )
        nearby = with_halo(packed, ((("region", "member"), 0),), tiles_here)
        ensemble = analyse(member_ship[p], nearby, ensemble)
    return lax.all_to_all(ensemble, "member", split_axis=0, concat_axis=1, tiled=True)


def solution(mesh):
    in_specs = (
        P("member", "region"),
        P("region"),
        P(None, None, ("region", "member"), None),
        P(None, None, ("region", "member"), None),
        P(None, None, ("region", "member"), None),
        P(None, None, ("region", "member"), None),
        P(None, None, ("region", "member")),
    )
    out_specs = P("member", "region")
    return jax.shard_map(local, mesh=mesh, in_specs=in_specs, out_specs=out_specs, check_vma=False)
```

profile of v0, /device:TPU:1, one launch (start us, length us, event | category | flops | bytes accessed | tf_op | source)
XLA Modules:
  0.0 133.5 jit_solution(1573497818909304085)
XLA Ops:
  1.7 2.6 %collective-permute-start = (f32[40,8]{1,0:T(8,128)S(1)}, f32[40,8]{1,0:T(8,128)S(1)}, u32[]{:S(2)}, u32[]{:S(2)}) collective-permute-start(f32[40,8]{1,0:T(8,128)S(1)} %pad_maximum_fusion.5), channel_id=1, source_target_pairs={{0,8},{8,16},{16,24},{24,0},{1,9},{9,17},{17,25},{25,1},{2,10},{10... | collective-permute-start | bytes 3848 | tf_op jit(solution)/shard_map/ppermute | solution.py:51
  4.3 1.4 %collective-permute-done.1 = f32[40,4]{1,0:T(8,128)S(1)} collective-permute-done((f32[40,4]{1,0:T(8,128)S(1)}, f32[40,4]{1,0:T(8,128)S(1)}, u32[]{:S(2)}, u32[]{:S(2)}) %collective-permute-start.1) | collective-permute-done | bytes 672 | tf_op jit(solution)/shard_map/ppermute | solution.py:52
  6.8 0.9 fusion.11
  7.7 0.9 fusion.7
  8.6 0.9 fusion.3
  10.4 1.0 copy.30
  11.4 5.7 %all-to-all-start = ((f32[32,8,1024]{2,0,1:T(8,128)}), f32[32,8,1024]{2,0,1:T(8,128)S(1)}, u32[]{:S(2)}, u32[]{:S(2)}) async-start(f32[32,8,1024]{2,0,1:T(8,128)} %bitcast.65), calls=%async_computation | async-start | bytes 2097152 | tf_op jit(solution)/shard_map/all_to_all | solution.py:191
  17.4 23.9 %all-to-all-done = f32[32,8,1024]{2,0,1:T(8,128)S(1)} async-done(((f32[32,8,1024]{2,0,1:T(8,128)}), f32[32,8,1024]{2,0,1:T(8,128)S(1)}, u32[]{:S(2)}, u32[]{:S(2)}) %all-to-all-start) | async-done | bytes 1048608 | tf_op jit(solution)/shard_map/all_to_all | solution.py:191
  41.6 1.0 gather_fusion
  42.9 2.4 %collective-permute-start.2 = (f32[2,257,128]{2,1,0:T(8,128)S(1)}, f32[2,257,128]{2,1,0:T(8,128)S(1)}, u32[]{:S(2)}, u32[]{:S(2)}) collective-permute-start(f32[2,257,128]{2,1,0:T(8,128)S(1)} %pad_maximum_fusion.2), channel_id=1, source_target_pairs={{0,1},{1,2},{2,3},{3,4},{4,5},{5,6},{6,7},{7,8},{8,9},{9,10},{10,1... | collective-permute-start | bytes 789512 | tf_op jit(solution)/shard_map/ppermute | solution.py:28
  45.3 2.2 %collective-permute-start.3 = (f32[2,257,128]{2,1,0:T(8,128)S(1)}, f32[2,257,128]{2,1,0:T(8,128)S(1)}, u32[]{:S(2)}, u32[]{:S(2)}) collective-permute-start(f32[2,257,128]{2,1,0:T(8,128)S(1)} %pad_maximum_fusion.2), channel_id=1, source_target_pairs={{1,0},{2,1},{3,2},{4,3},{5,4},{6,5},{7,6},{8,7},{9,8},{10,9},{11,1... | collective-permute-start | bytes 789512 | tf_op jit(solution)/shard_map/ppermute | solution.py:30
  48.1 8.2 %collective-permute-done.2 = f32[2,257,128]{2,1,0:T(8,128)S(1)} collective-permute-done((f32[2,257,128]{2,1,0:T(8,128)S(1)}, f32[2,257,128]{2,1,0:T(8,128)S(1)}, u32[]{:S(2)}, u32[]{:S(2)}) %collective-permute-start.2) | collective-permute-done | bytes 263200 | tf_op jit(solution)/shard_map/ppermute | solution.py:28
  56.3 2.2 %collective-permute-done.3 = f32[2,257,128]{2,1,0:T(8,128)S(1)} collective-permute-done((f32[2,257,128]{2,1,0:T(8,128)S(1)}, f32[2,257,128]{2,1,0:T(8,128)S(1)}, u32[]{:S(2)}, u32[]{:S(2)}) %collective-permute-start.3) | collective-permute-done | bytes 263200 | tf_op jit(solution)/shard_map/ppermute | solution.py:30
  58.4 1.0 pad_maximum_fusion.tiles_ref
  59.4 12.9 %shard_map.73.ens_ref = f32[256,1024]{1,0:T(8,128)} custom-call(f32[2,6]{1,0:T(2,128)} %get-tuple-element.10.member_ref, f32[6,257,128]{2,1,0:T(8,128)} %pad_maximum_fusion.tiles_ref, f32[256,1024]{1,0:T(8,128)} %bitcast.67), custom_call_target="tpu_custom_call" | custom-call | tf_op jit(solution)/shard_map/pallas_call | solution.py:148
  72.3 1.6 %copy.24 = f32[256,1024]{0,1:T(8,128)S(1)} copy(f32[256,1024]{1,0:T(8,128)} %shard_map.73.ens_ref) | data formatting | bytes 2097152 | tf_op jit(solution)/shard_map/pallas_call | solution.py:148
  73.9 1.0 gather_fusion.1
  75.7 4.4 %collective-permute-start.5 = (f32[2,257,128]{2,1,0:T(8,128)S(1)}, f32[2,257,128]{2,1,0:T(8,128)S(1)}, u32[]{:S(2)}, u32[]{:S(2)}) collective-permute-start(f32[2,257,128]{2,1,0:T(8,128)S(1)} %pad_maximum_fusion.3), channel_id=1, source_target_pairs={{1,0},{2,1},{3,2},{4,3},{5,4},{6,5},{7,6},{8,7},{9,8},{10,9},{11,1... | collective-permute-start | bytes 789512 | tf_op jit(solution)/shard_map/ppermute | solution.py:30
  80.1 5.8 %collective-permute-done.4 = f32[2,257,128]{2,1,0:T(8,128)S(1)} collective-permute-done((f32[2,257,128]{2,1,0:T(8,128)S(1)}, f32[2,257,128]{2,1,0:T(8,128)S(1)}, u32[]{:S(2)}, u32[]{:S(2)}) %collective-permute-start.4) | collective-permute-done | bytes 263200 | tf_op jit(solution)/shard_map/ppermute | solution.py:28
  85.9 2.3 %collective-permute-done.5 = f32[2,257,128]{2,1,0:T(8,128)S(1)} collective-permute-done((f32[2,257,128]{2,1,0:T(8,128)S(1)}, f32[2,257,128]{2,1,0:T(8,128)S(1)}, u32[]{:S(2)}, u32[]{:S(2)}) %collective-permute-start.5) | collective-permute-done | bytes 263200 | tf_op jit(solution)/shard_map/ppermute | solution.py:30
  88.2 1.0 pad_maximum_fusion.1.tiles_ref
  89.2 12.9 %shard_map.74 = f32[256,1024]{1,0:T(8,128)} custom-call(f32[2,6]{1,0:T(2,128)} %get-tuple-element.11.member_ref, f32[6,257,128]{2,1,0:T(8,128)} %pad_maximum_fusion.1.tiles_ref, f32[256,1024]{1,0:T(8,128)} %shard_map.73.ens_ref), custom_call_target="tpu_custom_call" | custom-call | tf_op jit(solution)/shard_map/pallas_call | solution.py:148
  102.1 30.4 %all_to_all.38 = f32[8,32,1024]{2,1,0:T(8,128)S(1)} all-to-all(f32[8,32,1024]{2,1,0:T(8,128)} %bitcast.69), channel_id=1, replica_groups=mesh['region'=4,'member'=8] {'member'}, dimensions={0} | all-to-all | bytes 2097152 | tf_op jit(solution)/shard_map/all_to_all | solution.py:198
  132.4 1.1 copy.28
  (55 shorter events, 5.8 us)
Async XLA Ops:
  0.0 1.6 %copy-start = (f32[32,8192]{1,0:T(8,128)S(1)}, f32[32,8192]{1,0:T(8,128)}, u32[]{:S(2)}) copy-start(f32[32,8192]{1,0:T(8,128)} %param.7) | copy-start | bytes 3145732
  0.9 4.8 %copy-start.2 = (f32[8192]{0:T(1024)S(1)}, f32[8192]{0:T(1024)}, u32[]{:S(2)}) copy-start(f32[8192]{0:T(1024)} %param.8) | copy-start | bytes 98308
  1.6 4.1 %collective-permute-start.1 = (f32[40,4]{1,0:T(8,128)S(1)}, f32[40,4]{1,0:T(8,128)S(1)}, u32[]{:S(2)}, u32[]{:S(2)}) collective-permute-start(f32[40,4]{1,0:T(8,128)S(1)} %pad_maximum_fusion.4), channel_id=1, source_target_pairs={{8,0},{16,8},{24,16},{0,24},{9,1},{17,9},{25,17},{1,25},{10,2},{18... | collective-permute-start | bytes 1928 | tf_op jit(solution)/shard_map/ppermute | solution.py:52
  1.7 4.0 %collective-permute-start = (f32[40,8]{1,0:T(8,128)S(1)}, f32[40,8]{1,0:T(8,128)S(1)}, u32[]{:S(2)}, u32[]{:S(2)}) collective-permute-start(f32[40,8]{1,0:T(8,128)S(1)} %pad_maximum_fusion.5), channel_id=1, source_target_pairs={{0,8},{8,16},{16,24},{24,0},{1,9},{9,17},{17,25},{25,1},{2,10},{10... | collective-permute-start | bytes 3848 | tf_op jit(solution)/shard_map/ppermute | solution.py:51
  11.4 5.7 %copy-start.5 = (s32[1,2,2,128]{3,2,1,0:T(2,128)S(1)}, s32[1,2,2,128]{3,2,1,0:T(2,128)}, u32[]{:S(2)}) copy-start(s32[1,2,2,128]{3,2,1,0:T(2,128)} %param.9) | copy-start | bytes 6148
  11.4 5.7 %copy-start.7 = (s32[1,2,2]{2,1,0:T(2,128)S(1)}, s32[1,2,2]{2,1,0:T(2,128)}, u32[]{:S(2)}) copy-start(s32[1,2,2]{2,1,0:T(2,128)} %param.13) | copy-start | bytes 52
  11.4 5.8 %copy-start.6 = (s32[1,2,2,4]{3,2,1,0:T(2,128)S(1)}, s32[1,2,2,4]{3,2,1,0:T(2,128)}, u32[]{:S(2)}) copy-start(s32[1,2,2,4]{3,2,1,0:T(2,128)} %param.12) | copy-start | bytes 196
  11.4 5.9 %copy-start.3 = (f32[1,2,2,128]{3,2,1,0:T(2,128)S(1)}, f32[1,2,2,128]{3,2,1,0:T(2,128)}, u32[]{:S(2)}) copy-start(f32[1,2,2,128]{3,2,1,0:T(2,128)} %param.11) | copy-start | bytes 6148
  11.4 29.8 %all-to-all-start = ((f32[32,8,1024]{2,0,1:T(8,128)}), f32[32,8,1024]{2,0,1:T(8,128)S(1)}, u32[]{:S(2)}, u32[]{:S(2)}) async-start(f32[32,8,1024]{2,0,1:T(8,128)} %bitcast.65), calls=%async_computation | async-start | bytes 2097152 | tf_op jit(solution)/shard_map/all_to_all | solution.py:191
  41.3 1.3 copy-start.1
  41.6 1.2 copy-start.4
  42.9 13.4 %collective-permute-start.2 = (f32[2,257,128]{2,1,0:T(8,128)S(1)}, f32[2,257,128]{2,1,0:T(8,128)S(1)}, u32[]{:S(2)}, u32[]{:S(2)}) collective-permute-start(f32[2,257,128]{2,1,0:T(8,128)S(1)} %pad_maximum_fusion.2), channel_id=1, source_target_pairs={{0,1},{1,2},{2,3},{3,4},{4,5},{5,6},{6,7},{7,8},{8,9},{9,10},{10,1... | collective-permute-start | bytes 789512 | tf_op jit(solution)/shard_map/ppermute | solution.py:28
  45.3 13.2 %collective-permute-start.3 = (f32[2,257,128]{2,1,0:T(8,128)S(1)}, f32[2,257,128]{2,1,0:T(8,128)S(1)}, u32[]{:S(2)}, u32[]{:S(2)}) collective-permute-start(f32[2,257,128]{2,1,0:T(8,128)S(1)} %pad_maximum_fusion.2), channel_id=1, source_target_pairs={{1,0},{2,1},{3,2},{4,3},{5,4},{6,5},{7,6},{8,7},{9,8},{10,9},{11,1... | collective-permute-start | bytes 789512 | tf_op jit(solution)/shard_map/ppermute | solution.py:30
  74.9 0.7 slice-start
  75.6 10.3 %collective-permute-start.4 = (f32[2,257,128]{2,1,0:T(8,128)S(1)}, f32[2,257,128]{2,1,0:T(8,128)S(1)}, u32[]{:S(2)}, u32[]{:S(2)}) collective-permute-start(f32[2,257,128]{2,1,0:T(8,128)S(1)} %pad_maximum_fusion.3), channel_id=1, source_target_pairs={{0,1},{1,2},{2,3},{3,4},{4,5},{5,6},{6,7},{7,8},{8,9},{9,10},{10,1... | collective-permute-start | bytes 789512 | tf_op jit(solution)/shard_map/ppermute | solution.py:28
  75.7 12.5 %collective-permute-start.5 = (f32[2,257,128]{2,1,0:T(8,128)S(1)}, f32[2,257,128]{2,1,0:T(8,128)S(1)}, u32[]{:S(2)}, u32[]{:S(2)}) collective-permute-start(f32[2,257,128]{2,1,0:T(8,128)S(1)} %pad_maximum_fusion.3), channel_id=1, source_target_pairs={{1,0},{2,1},{3,2},{4,3},{5,4},{6,5},{7,6},{8,7},{9,8},{10,9},{11,1... | collective-permute-start | bytes 789512 | tf_op jit(solution)/shard_map/ppermute | solution.py:30
where the time goes:
time: 136 us; the launch traced here: 134 us
  waiting for transfers between devices  43.7 us (32%)
  blocking collectives  30.4 us (22%)
  Pallas kernels  25.8 us (19%)
  starting transfers between devices  17.4 us (13%)
  local copies, waits for them, and re-layouts  9.23 us (7%)
  other arithmetic  6.78 us (5%)
    all_to_all x1, blocking collectives, local(): lax.all_to_all(ensemble, 'member', split_axis=0, concat_axis=1, tiled=True)  30.4 us
    pallas_call x2, Pallas kernels, analyse(): pl.pallas_call(analysis_kernel, out_shape=jax.ShapeDtypeStruct(ensemble.s...  25.8 us
    all_to_all x1, waiting for transfers between devices, local(): lax.all_to_all(replica, 'member', split_axis=1, concat_axis=0, tiled=True)  23.9 us
    ppermute x2, waiting for transfers between devices, with_halo(): lax.ppermute(tail, axis, [(i, (i + 1) % count) for i in range(count)])  14 us
    ppermute x2, starting transfers between devices, with_halo(): lax.ppermute(head, axis, [((i + 1) % count, i) for i in range(count)])  6.64 us
    all_to_all x1, starting transfers between devices, local(): lax.all_to_all(replica, 'member', split_axis=1, concat_axis=0, tiled=True)  5.67 us
    ppermute x2, waiting for transfers between devices, with_halo(): lax.ppermute(head, axis, [((i + 1) % count, i) for i in range(count)])  4.46 us
    add x4, other arithmetic, forecast(): wide[:, 2:inner + 2]  3.55 us
  transfers between devices with their start and end apart: 7, of which 6 were waited for; matrix products, arithmetic and copies ran while one was open for 1% of the time, Pallas kernels for 0%

commit v1 on v0

v1 whole, which is shorter than its diff:
```python
import functools
import math

import jax
import jax.numpy as jnp
from jax import lax
from jax.experimental import pallas as pl
from jax.experimental.pallas import tpu as pltpu
from jax.sharding import PartitionSpec as P

BLOCK = 512
NS_ITERS = 10
STEPS = 4
PASSES = 2
LANES = 128
MESH = pl.DeviceIdType.MESH

time_step = 0.05


def split(value):
    high = value.astype(jnp.bfloat16)
    low = (value - high.astype(jnp.float32)).astype(jnp.bfloat16)
    return high, low


def dot3(left, right, contract=((1,), (0,))):
    wide = jnp.concatenate([left[0], left[0], left[1]], axis=contract[0][0])
    deep = jnp.concatenate([right[0], right[1], right[0]], axis=contract[1][0])
    return lax.dot_general(wide, deep, (contract, ((), ())), preferred_element_type=jnp.float32)


def roots(systems, identity):
    frobs = [jnp.sqrt(jnp.sum(s * s, keepdims=True)) for s in systems]
    firsts = [s / f for s, f in zip(systems, frobs)]

    def quartic(error):
        halves = split(error)
        square = dot3(halves, halves)
        rest = 0.375 * identity + 0.3125 * error + 0.0625 * square
        return 0.5 * error + dot3(split(square), split(rest))

    def close(inv, root):
        return identity - dot3(split(inv), split(root))

    invs, rts, errors = [], [], []
    for first in firsts:
        q = quartic(identity - first)
        invs.append(identity + q)
        rts.append(first + dot3(split(first), split(q)))
    errors = [close(i, r) for i, r in zip(invs, rts)]
    count = len(systems)

    def step(_, state):
        invs, rts, errors = state
        qs = [split(quartic(e)) for e in errors]
        invs = [i + dot3(split(i), q) for i, q in zip(invs, qs)]
        rts = [r + dot3(split(r), q) for r, q in zip(rts, qs)]
        return invs, rts, [close(i, r) for i, r in zip(invs, rts)]

    invs, rts, errors = lax.fori_loop(0, NS_ITERS // 2 - 2, step, (invs, rts, errors))
    qs = [split(quartic(e)) for e in errors]
    invs = [i + dot3(split(i), q) for i, q in zip(invs, qs)]
    return [i / jnp.sqrt(f) for i, f in zip(invs, frobs)]


def memberships(listed, counts, device, devices, tiles_here):
    slot_ids = (listed - (device - 1) * tiles_here) % (devices * tiles_here)
    living = lax.broadcasted_iota(jnp.int32, listed.shape, 2) < counts[:, :, None]
    candidates = lax.broadcasted_iota(jnp.int32, (1, 1, 1, 3 * tiles_here), 3)
    chosen = living[..., None] & (slot_ids[..., None] == candidates)
    return jnp.sum(chosen.astype(jnp.float32), axis=2)


def snake_member(position, count):
    half = count // 2
    late = position // half
    return 2 * position * (1 - late) + (2 * (count - 1 - position) + 1) * late


def snake_position(member, count):
    odd = member % 2
    return (member // 2) * (1 - odd) + (count - 1 - member // 2) * odd


def forecast_window(wide, forcing):
    width = wide.shape[1]
    for _ in range(STEPS):
        ahead_one = pltpu.roll(wide, width - 1, 1)
        behind = pltpu.roll(wide, 1, 1)
        further = pltpu.roll(wide, 2, 1)
        wide = wide + time_step * ((ahead_one - further) * behind - wide + forcing)
    return wide[:, LANES : width - LANES]


def kernel(
    count,
    regions,
    x_ref,
    drive_ref,
    obs_ref,
    out_ref,
    fc_ref,
    ens_ref,
    upd_ref,
    left_ref,
    right_ref,
    dleft_ref,
    dright_ref,
    own_obs,
    tiles_ref,
    halo_send,
    halo_recv,
    obs_send,
    obs_recv,
    in_send,
    in_recv,
    tile_send,
    tile_recv,
    out_send,
    out_recv,
    local_sem,
):
    region = lax.axis_index("region")
    me = lax.axis_index("member")
    position = snake_position(me, count)
    rows, cells = x_ref.shape
    members = ens_ref.shape[0]
    window = ens_ref.shape[1]
    up = (region + 1) % regions
    down = (region + regions - 1) % regions
    nxt = (
        (region + (position + 1) // count) % regions,
        snake_member((position + 1) % count, count),
    )
    before = (position + count - 1) % count
    prv = (
        (region + regions - (count - position) // count) % regions,
        snake_member(before, count),
    )

    barrier = pltpu.get_barrier_semaphore()

    def greet(target):
        pl.semaphore_signal(barrier, inc=1, device_id=target, device_id_type=MESH)

    for k in range(1, count):
        greet((region, (me + k) % count))
    for target in ((up, me), (down, me), nxt, prv):
        greet(target)
    pl.semaphore_wait(barrier, count + 3)

    def remote(source, target, send, recv, device):
        return pltpu.make_async_remote_copy(
            src_ref=source,
            dst_ref=target,
            send_sem=send,
            recv_sem=recv,
            device_id=device,
            device_id_type=MESH,
        )

    last = slice(cells - LANES, cells)
    halos = [
        remote(x_ref.at[:, last], left_ref, halo_send.at[0], halo_recv.at[0], (up, me)),
        remote(x_ref.at[:, 0:LANES], right_ref, halo_send.at[1], halo_recv.at[1], (down, me)),
        remote(drive_ref.at[:, last], dleft_ref, halo_send.at[2], halo_recv.at[2], (up, me)),
        remote(drive_ref.at[:, 0:LANES], dright_ref, halo_send.at[3], halo_recv.at[3], (down, me)),
    ]
    for copy in halos:
        copy.start()

    obs_home = snake_member(me, count)
    obs_copy = remote(obs_ref, own_obs, obs_send, obs_recv, (region, obs_home))
    obs_local = pltpu.make_async_copy(obs_ref, own_obs, local_sem.at[0])

    @pl.when(obs_home != me)
    def _():
        obs_copy.start()

    @pl.when(obs_home == me)
    def _():
        obs_local.start()

    my_rows = pl.ds(pl.multiple_of(me * rows, 8), rows)

    def in_copy(w):
        return remote(
            fc_ref.at[:, pl.ds(pl.multiple_of(w * window, LANES), window)],
            ens_ref.at[my_rows, :],
            in_send.at[w],
            in_recv.at[me],
            (region, snake_member(w, count)),
        )

    def own_window():
        return pltpu.make_async_copy(
            fc_ref.at[:, pl.ds(pl.multiple_of(position * window, LANES), window)],
            ens_ref.at[my_rows, :],
            local_sem.at[1],
        )

    def ship(w):
        @pl.when(w != position)
        def _():
            in_copy(w).start()

        @pl.when(w == position)
        def _():
            own_window().start()

    quarter = max(count // 4, 1)
    outer = ((position + quarter) // (2 * quarter)) % 2
    first = quarter * (1 + 2 * outer) - 1

    def interior(k, carry):
        w = 1 + (first + k) % (count - 2)
        span = pl.ds(pl.multiple_of(w * window - LANES, LANES), window + 2 * LANES)
        fc_ref[:, pl.ds(pl.multiple_of(w * window, LANES), window)] = forecast_window(
            x_ref[:, span], drive_ref[:, span]
        )
        ship(w)
        return carry

    lax.fori_loop(0, count - 2, interior, 0)
    for copy in halos:
        copy.wait()
    head = window + LANES
    fc_ref[:, 0:window] = forecast_window(
        jnp.concatenate([left_ref[...], x_ref[:, 0:head]], axis=1),
        jnp.concatenate([dleft_ref[...], drive_ref[:, 0:head]], axis=1),
    )
    ship(0)
    fc_ref[:, cells - window : cells] = forecast_window(
        jnp.concatenate([x_ref[:, cells - head : cells], right_ref[...]], axis=1),
        jnp.concatenate([drive_ref[:, cells - head : cells], dright_ref[...]], axis=1),
    )
    ship(count - 1)

    @pl.when(obs_home != me)
    def _():
        obs_copy.wait()

    @pl.when(obs_home == me)
    def _():
        obs_local.wait()

    own_window().wait()

    for k in range(1, count):
        sender = (me + k) % count
        remote(
            fc_ref.at[:, 0:window],
            ens_ref.at[pl.ds(pl.multiple_of(sender * rows, 8), rows), :],
            in_send.at[0],
            in_recv.at[sender],
            (region, sender),
        ).wait_recv()

    def sent_in(k, carry):
        in_copy((position + k) % count).wait_send()
        return carry

    lax.fori_loop(1, count, sent_in, 0)

    eye_rows = lax.broadcasted_iota(jnp.int32, (members, members), 0)
    eye_columns = lax.broadcasted_iota(jnp.int32, (members, members), 1)
    identity = (eye_rows == eye_columns).astype(jnp.float32)
    tiles = tiles_ref.shape[3] // LANES
    blocks = window // BLOCK
    place = lax.broadcasted_iota(jnp.int32, (window, LANES), 0)

    def obs_row(kind, p, t):
        r = (kind * PASSES + p) * tiles + t
        return own_obs[r : r + 1, :]

    def exchange(p):
        state = ens_ref[...]
        high, rest = split_rest(state)
        middle, rest = split_rest(rest)
        low = rest.astype(jnp.bfloat16)
        chosen = jnp.concatenate(
            [
                (place == obs_row(0, p, t).astype(jnp.int32)).astype(jnp.bfloat16)
                for t in range(tiles)
            ],
            axis=1,
        )

        def pick(part):
            return jnp.dot(part, chosen, preferred_element_type=jnp.float32)

        picked = pick(high) + (pick(middle) + pick(low))
        center = jnp.mean(picked, axis=0, keepdims=True)
        values = jnp.concatenate([obs_row(1, p, t) for t in range(tiles)], axis=1)
        weights = jnp.concatenate([obs_row(2, p, t) for t in range(tiles)], axis=1)
        root_weight = jnp.sqrt(weights)
        tiles_ref[p, 1, 0:members, :] = (picked - center) * root_weight
        tiles_ref[p, 1, members : members + 8, :] = jnp.broadcast_to(
            (values - center) * root_weight, (8, values.shape[1])
        )
        copies = [
            remote(
                tiles_ref.at[p, 1], tiles_ref.at[p, 0], tile_send.at[p, 0], tile_recv.at[p, 0], nxt
            ),
            remote(
                tiles_ref.at[p, 1], tiles_ref.at[p, 2], tile_send.at[p, 1], tile_recv.at[p, 1], prv
            ),
        ]
        for copy in copies:
            copy.start()
        return copies

    def gather_systems(p, copies):
        grams = [(members - 1.0) * identity for _ in range(blocks)]
        pulls = [jnp.zeros((members, 1), jnp.float32) for _ in range(blocks)]
        for owner in (1, 0, 2):
            if owner == 0:
                for copy in copies:
                    copy.wait()
            for t in range(tiles):
                lanes = slice(t * LANES, (t + 1) * LANES)
                spread = tiles_ref[p, owner, 0:members, lanes]
                innovation = tiles_ref[p, owner, members : members + 1, lanes]
                halves = split(spread)
                gram = dot3(halves, halves, ((1,), (1,)))
                pull = jnp.sum(spread * innovation, axis=1, keepdims=True)
                slot = owner * tiles + t
                for b in range(blocks):
                    weight = obs_row(3, p, b)[:, slot : slot + 1]
                    grams[b] = grams[b] + weight * gram
                    pulls[b] = pulls[b] + weight * pull
        return grams, pulls

    def apply(inv_root, pull, b):
        inner = jnp.sum(inv_root * pull, axis=0, keepdims=True)
        shift = jnp.sum(inv_root * inner, axis=1, keepdims=True)
        state = ens_ref[:, b * BLOCK : (b + 1) * BLOCK]
        center = jnp.mean(state, axis=0, keepdims=True)
        anomaly = state - center
        base = center + jnp.sum(shift * anomaly, axis=0, keepdims=True)
        scaled = split(math.sqrt(members - 1) * inv_root)
        return base + dot3(scaled, split(anomaly))

    for p in range(PASSES - 1):
        grams, pulls = gather_systems(p, exchange(p))
        inv_roots = roots(grams, identity)
        for b in range(blocks):
            ens_ref[:, b * BLOCK : (b + 1) * BLOCK] = apply(inv_roots[b], pulls[b], b)

    def out_copy(b, k):
        target = (me + k) % count
        return remote(
            upd_ref.at[
                pl.ds(pl.multiple_of(target * rows, 8), rows), b * BLOCK : (b + 1) * BLOCK
            ],
            out_ref.at[:, pl.ds(pl.multiple_of(position * window + b * BLOCK, LANES), BLOCK)],
            out_send.at[b, k],
            out_recv.at[b, me],
            (region, target),
        )

    def out_own(b):
        return pltpu.make_async_copy(
            upd_ref.at[my_rows, b * BLOCK : (b + 1) * BLOCK],
            out_ref.at[:, pl.ds(pl.multiple_of(position * window + b * BLOCK, LANES), BLOCK)],
            local_sem.at[2 + b],
        )

    p = PASSES - 1
    grams, pulls = gather_systems(p, exchange(p))
    order = [(count // 2 + k) % count for k in range(count)]
    for b in range(blocks):
        (inv_root,) = roots([grams[b]], identity)
        upd_ref[:, b * BLOCK : (b + 1) * BLOCK] = apply(inv_root, pulls[b], b)
        for k in order:
            if k:
                out_copy(b, k).start()
        out_own(b).start()
    for b in range(blocks):
        for k in range(1, count):
            sender = (me + k) % count
            remote(
                upd_ref.at[0:rows, b * BLOCK : (b + 1) * BLOCK],
                out_ref.at[
                    :,
                    pl.ds(
                        pl.multiple_of(
                            snake_position(sender, count) * window + b * BLOCK, LANES
                        ),
                        BLOCK,
                    ),
                ],
                out_send.at[b, 0],
                out_recv.at[b, sender],
                (region, sender),
            ).wait_recv()
        for k in range(1, count):
            out_copy(b, k).wait_send()
        out_own(b).wait()


def split_rest(value):
    high = value.astype(jnp.bfloat16)
    return high, value - high.astype(jnp.float32)


def local(
    initial_ensemble,
    driving_term,
    observation_cells,
    observation_values,
    observation_weight,
    block_tile_list,
    block_tile_count,
):
    count = lax.axis_size("member")
    regions = lax.axis_size("region")
    device = lax.axis_index("region") * count + lax.axis_index("member")
    tiles_here = observation_cells.shape[2]
    rows, cells = initial_ensemble.shape
    members = rows * count
    window = cells // count
    blocks = window // BLOCK
    member_ship = memberships(
        block_tile_list[0], block_tile_count[0], device, count * regions, tiles_here
    )
    slots = member_ship.shape[2]
    obs = jnp.concatenate(
        [
            observation_cells[0].astype(jnp.float32).reshape(-1, LANES),
            observation_values[0].reshape(-1, LANES),
            observation_weight[0].reshape(-1, LANES),
            jnp.pad(member_ship.reshape(-1, slots), ((0, 0), (0, LANES - slots))),
        ]
    )
    vmem = pl.BlockSpec(memory_space=pltpu.VMEM)
    f32 = jnp.float32
    dma = pltpu.SemaphoreType.DMA
    return pl.pallas_call(
        functools.partial(kernel, count, regions),
        out_shape=jax.ShapeDtypeStruct((rows, cells), f32),
        in_specs=[vmem, vmem, vmem],
        out_specs=vmem,
        scratch_shapes=[
            pltpu.VMEM((rows, cells), f32),
            pltpu.VMEM((members, window), f32),
            pltpu.VMEM((members, window), f32),
            pltpu.VMEM((rows, LANES), f32),
            pltpu.VMEM((rows, LANES), f32),
            pltpu.VMEM((1, LANES), f32),
            pltpu.VMEM((1, LANES), f32),
            pltpu.VMEM(obs.shape, f32),
            pltpu.VMEM((PASSES, 3, members + 8, tiles_here * LANES), f32),
            dma((4,)),
            dma((4,)),
            dma,
            dma,
            dma((count,)),
            dma((count,)),
            dma((PASSES, 2)),
            dma((PASSES, 2)),
            dma((blocks, count)),
            dma((blocks, count)),
            dma((2 + blocks,)),
        ],
        compiler_params=pltpu.CompilerParams(
            collective_id=0, has_side_effects=True, vmem_limit_bytes=48 * 1024 * 1024
        ),
    )(initial_ensemble, driving_term[None], obs)


def solution(mesh):
    in_specs = (
        P("member", "region"),
        P("region"),
        P(None, None, ("region", "member"), None),
        P(None, None, ("region", "member"), None),
        P(None, None, ("region", "member"), None),
        P(None, None, ("region", "member"), None),
        P(None, None, ("region", "member")),
    )
    out_specs = P("member", "region")
    return jax.shard_map(local, mesh=mesh, in_specs=in_specs, out_specs=out_specs, check_vma=False)
```

time: 136 us -> 93.7 us (0.69); the launches traced: 134 us -> 92.6 us
  Pallas kernels: 25.8 us -> 87.6 us
  waiting for transfers between devices: 43.7 us -> 0 us
  blocking collectives: 30.4 us -> 0 us
  starting transfers between devices: 17.4 us -> 0 us
  local copies, waits for them, and re-layouts: 9.23 us -> 3.48 us
  other arithmetic: 6.78 us -> 1.56 us
    pallas_call x2 -> x1, Pallas kernels: 25.8 us -> 87.6 us  [local(): pl.pallas_call(functools.partial(kernel, count, regions), out_shape=jax.S...]
    all_to_all x1 -> x0, blocking collectives: 30.4 us -> none  [local(): lax.all_to_all(ensemble, 'member', split_axis=0, concat_axis=1, tiled=True)]
    all_to_all x1 -> x0, waiting for transfers between devices: 23.9 us -> none  [local(): lax.all_to_all(replica, 'member', split_axis=1, concat_axis=0, tiled=True)]
    ppermute x6 -> x0, waiting for transfers between devices: 19.8 us -> none  [the longest x2 14 us: with_halo(): lax.ppermute(tail, axis, [(i, (i + 1) % count) for i in range(count)])]
    ppermute x6 -> x0, starting transfers between devices: 11.7 us -> none  [the longest x2 6.64 us: with_halo(): lax.ppermute(head, axis, [((i + 1) % count, i) for i in range(count)])]
    all_to_all x1 -> x0, starting transfers between devices: 5.67 us -> none  [local(): lax.all_to_all(replica, 'member', split_axis=1, concat_axis=0, tiled=True)]
    add x4 -> x0, other arithmetic: 3.55 us -> none  [forecast(): wide[:, 2:inner + 2]]
    unnamed x16 -> x11, local copies, waits for them, and re-layouts: 0.03 us -> 3.48 us
  transfers between devices with their start and end apart: 7 -> 0, of which waited for: 6 -> 0; matrix products, arithmetic and copies ran while one was open for 1% -> 0% of each run, Pallas kernels for 0% -> 0%
where the time goes in v1:
time: 93.7 us; the launch traced here: 92.6 us
  Pallas kernels  87.6 us (93%)
  local copies, waits for them, and re-layouts  3.48 us (4%)
  other arithmetic  1.56 us (2%)
    pallas_call x1, Pallas kernels, local(): pl.pallas_call(functools.partial(kernel, count, regions), out_shape=jax.S...  87.6 us
    unnamed x11, local copies, waits for them, and re-layouts  3.48 us

profile of v1, /device:TPU:1, one launch (start us, length us, event | category | flops | bytes accessed | tf_op | source)
XLA Modules:
  0.0 92.6 jit_solution(16861421273119155084)
XLA Ops:
  0.0 0.0 copy-start.1
  0.0 0.8 iota_compare_fusion.2
  0.8 0.7 and_select_fusion
  1.5 0.0 copy-start.2
  1.5 0.1 convert_reduce_fusion
  1.6 0.6 copy-done.2
  2.1 0.0 copy-start.3
  2.1 0.0 copy-start.4
  2.1 0.7 copy-done.3
  2.8 0.0 copy-done.4
  2.8 0.0 copy-done.1
  2.9 0.0 copy-start
  2.9 1.2 %copy-done = f32[32,8192]{1,0:T(8,128)S(1)} copy-done((f32[32,8192]{1,0:T(8,128)S(1)}, f32[32,8192]{1,0:T(8,128)}, u32[]{:S(2)}) %copy-start) | copy-done | bytes 1048600
  4.1 87.6 %shard_map.73 = f32[32,8192]{1,0:T(8,128)S(1)} custom-call(f32[32,8192]{1,0:T(8,128)S(1)} %copy-done, f32[1,8192]{1,0:T(1,128)S(1)} %bitcast.8, f32[16,128]{1,0:T(8,128)S(1)} %select_maximum_fusion.obs_ref), custom_call_target="tpu_custom_call" | custom-call | tf_op jit(solution)/shard_map/pallas_call | solution.py:440
  91.7 1.0 %copy.9 = f32[32,8192]{1,0:T(8,128)} copy(f32[32,8192]{1,0:T(8,128)S(1)} %shard_map.73) | data formatting | bytes 2097152
  (2 shorter events, 0.0 us)
Async XLA Ops:
  0.0 2.8 %copy-start.1 = (f32[8192]{0:T(1024)S(1)}, f32[8192]{0:T(1024)}, u32[]{:S(2)}) copy-start(f32[8192]{0:T(1024)} %param.8) | copy-start | bytes 98308
  1.5 0.7 copy-start.2
  2.1 0.7 copy-start.3
  2.1 0.7 copy-start.4
  2.9 1.2 %copy-start = (f32[32,8192]{1,0:T(8,128)S(1)}, f32[32,8192]{1,0:T(8,128)}, u32[]{:S(2)}) copy-start(f32[32,8192]{1,0:T(8,128)} %x_ref.1) | copy-start | bytes 3145732

commit v2 on v1

v2 whole, which is shorter than its diff:
```python
import functools
import math

import jax
import jax.numpy as jnp
from jax import lax
from jax.experimental import pallas as pl
from jax.experimental.pallas import tpu as pltpu
from jax.sharding import PartitionSpec as P

BLOCK = 512
NS_ITERS = 10
STEPS = 4
PASSES = 2
LANES = 128
MESH = pl.DeviceIdType.MESH

time_step = 0.05


def split(value):
    high = value.astype(jnp.bfloat16)
    low = (value - high.astype(jnp.float32)).astype(jnp.bfloat16)
    return high, low


def dot3(left, right, contract=((1,), (0,))):
    wide = jnp.concatenate([left[0], left[0], left[1]], axis=contract[0][0])
    deep = jnp.concatenate([right[0], right[1], right[0]], axis=contract[1][0])
    return lax.dot_general(wide, deep, (contract, ((), ())), preferred_element_type=jnp.float32)


def roots(systems, identity):
    frobs = [jnp.sqrt(jnp.sum(s * s, keepdims=True)) for s in systems]
    firsts = [s / f for s, f in zip(systems, frobs)]

    def quartic(error):
        halves = split(error)
        square = dot3(halves, halves)
        rest = 0.375 * identity + 0.3125 * error + 0.0625 * square
        return 0.5 * error + dot3(split(square), split(rest))

    def close(inv, root):
        return identity - dot3(split(inv), split(root))

    invs, rts, errors = [], [], []
    for first in firsts:
        q = quartic(identity - first)
        invs.append(identity + q)
        rts.append(first + dot3(split(first), split(q)))
    errors = [close(i, r) for i, r in zip(invs, rts)]
    count = len(systems)

    def step(_, state):
        invs, rts, errors = state
        qs = [split(quartic(e)) for e in errors]
        invs = [i + dot3(split(i), q) for i, q in zip(invs, qs)]
        rts = [r + dot3(split(r), q) for r, q in zip(rts, qs)]
        return invs, rts, [close(i, r) for i, r in zip(invs, rts)]

    invs, rts, errors = lax.fori_loop(0, NS_ITERS // 2 - 2, step, (invs, rts, errors))
    qs = [split(quartic(e)) for e in errors]
    invs = [i + dot3(split(i), q) for i, q in zip(invs, qs)]
    return [i / jnp.sqrt(f) for i, f in zip(invs, frobs)]


def snake_member(position, count):
    half = count // 2
    late = position // half
    return 2 * position * (1 - late) + (2 * (count - 1 - position) + 1) * late


def snake_position(member, count):
    odd = member % 2
    return (member // 2) * (1 - odd) + (count - 1 - member // 2) * odd


def forecast_window(wide, forcing):
    width = wide.shape[1]
    for _ in range(STEPS):
        ahead_one = pltpu.roll(wide, width - 1, 1)
        behind = pltpu.roll(wide, 1, 1)
        further = pltpu.roll(wide, 2, 1)
        wide = wide + time_step * ((ahead_one - further) * behind - wide + forcing)
    return wide[:, LANES : width - LANES]


def kernel(
    count,
    regions,
    x_ref,
    drive_ref,
    cells_ref,
    values_ref,
    weights_ref,
    list_ref,
    counts_ref,
    out_ref,
    held_ref,
    fc_ref,
    ens_ref,
    upd_ref,
    dheld_ref,
    own_cells,
    own_values,
    own_weights,
    own_list,
    own_counts,
    tiles_ref,
    load_sem,
    halo_send,
    halo_recv,
    obs_send,
    obs_recv,
    in_send,
    in_recv,
    tile_send,
    tile_recv,
    out_send,
    out_recv,
    local_sem,
):
    region = lax.axis_index("region")
    me = lax.axis_index("member")
    rows = fc_ref.shape[0]
    cells = fc_ref.shape[1]
    members = ens_ref.shape[0]
    window = ens_ref.shape[1]
    up = (region + 1) % regions
    down = (region + regions - 1) % regions
    base = region - region % 2
    across = 2 * count
    mine = 2 * snake_position(me, count) + region % 2
    source_region = base + mine // count
    position = mine % count
    offset = (region % 2) * count

    def host(place):
        return (base + place % 2, snake_member(place // 2, count))

    nxt_place = (mine + 1) % across
    nxt = (
        (base + 2 * ((mine + 1) // across) + nxt_place % 2) % regions,
        snake_member(nxt_place // 2, count),
    )
    prv_place = (mine + across - 1) % across
    prv = (
        (base + regions - 2 * ((across - mine) // across) + prv_place % 2) % regions,
        snake_member(prv_place // 2, count),
    )

    def load(w):
        span = pl.ds(pl.multiple_of(w * window, LANES), window)
        kept = pl.ds(pl.multiple_of(w * window + LANES, LANES), window)
        return pltpu.make_async_copy(x_ref.at[:, span], held_ref.at[:, kept], load_sem.at[w])

    def load_all(w, carry):
        load(w).start()
        return carry

    drive_load = pltpu.make_async_copy(
        drive_ref, dheld_ref.at[:, LANES : LANES + cells], local_sem.at[0]
    )
    drive_load.start()
    lax.fori_loop(0, count, load_all, 0)

    barrier = pltpu.get_barrier_semaphore()

    def greet(target):
        pl.semaphore_signal(barrier, inc=1, device_id=target, device_id_type=MESH)

    for k in range(count):
        greet((base + 1 - region % 2, (me + k) % count))
        if k:
            greet((region, (me + k) % count))
    for target in ((up, me), (down, me), nxt, prv):
        greet(target)
    pl.semaphore_wait(barrier, across + 3)

    def remote(source, target, send, recv, device):
        return pltpu.make_async_remote_copy(
            src_ref=source,
            dst_ref=target,
            send_sem=send,
            recv_sem=recv,
            device_id=device,
            device_id_type=MESH,
        )

    last = slice(cells - LANES, cells)
    end = LANES + cells
    halos = [
        remote(
            x_ref.at[:, last], held_ref.at[:, 0:LANES], halo_send.at[0], halo_recv.at[0], (up, me)
        ),
        remote(
            x_ref.at[:, 0:LANES],
            held_ref.at[:, end : end + LANES],
            halo_send.at[1],
            halo_recv.at[1],
            (down, me),
        ),
        remote(
            drive_ref.at[:, last],
            dheld_ref.at[:, 0:LANES],
            halo_send.at[2],
            halo_recv.at[2],
            (up, me),
        ),
        remote(
            drive_ref.at[:, 0:LANES],
            dheld_ref.at[:, end : end + LANES],
            halo_send.at[3],
            halo_recv.at[3],
            (down, me),
        ),
    ]
    for copy in halos:
        copy.start()

    obs_stays = (offset + me) == mine
    obs_pairs = (
        (cells_ref, own_cells),
        (values_ref, own_values),
        (weights_ref, own_weights),
        (list_ref, own_list),
        (counts_ref, own_counts),
    )
    obs_copies = [
        remote(source, target, obs_send.at[i], obs_recv.at[i], host(offset + me))
        for i, (source, target) in enumerate(obs_pairs)
    ]
    obs_locals = [
        pltpu.make_async_copy(source, target, obs_send.at[i])
        for i, (source, target) in enumerate(obs_pairs)
    ]

    @pl.when(jnp.logical_not(obs_stays))
    def _():
        for copy in obs_copies:
            copy.start()

    @pl.when(obs_stays)
    def _():
        for copy in obs_locals:
            copy.start()

    my_rows = pl.ds(pl.multiple_of(me * rows, 8), rows)

    def in_copy(w):
        return remote(
            fc_ref.at[:, pl.ds(pl.multiple_of(w * window, LANES), window)],
            ens_ref.at[my_rows, :],
            in_send.at[w],
            in_recv.at[me],
            host(offset + w),
        )

    def own_window():
        return pltpu.make_async_copy(
            fc_ref.at[:, pl.ds(pl.multiple_of(position * window, LANES), window)],
            ens_ref.at[my_rows, :],
            local_sem.at[1],
        )

    def ship(w):
        @pl.when(offset + w != mine)
        def _():
            in_copy(w).start()

        @pl.when(offset + w == mine)
        def _():
            own_window().start()

    def forecast_at(w):
        wide = pl.ds(pl.multiple_of(w * window, LANES), window + 2 * LANES)
        fc_ref[:, pl.ds(pl.multiple_of(w * window, LANES), window)] = forecast_window(
            held_ref[:, wide], dheld_ref[:, wide]
        )
        ship(w)

    def loaded(w, carry):
        load(w).wait()
        return carry

    def interior(k, carry):
        forecast_at(1 + (first + k) % (count - 2))
        return carry

    quarter = max(count // 4, 1)
    near = snake_position(me, count)
    outer = ((near + quarter) // (2 * quarter)) % 2
    first = (count // 2 - 1) * ((outer + region + 1) % 2)
    drive_load.wait()
    lax.fori_loop(0, count, loaded, 0)
    lax.fori_loop(0, count - 2, interior, 0)
    for copy in halos:
        copy.wait()
    forecast_at(0)
    forecast_at(count - 1)

    @pl.when(jnp.logical_not(obs_stays))
    def _():
        for copy in obs_copies:
            copy.wait()

    @pl.when(obs_stays)
    def _():
        for copy in obs_locals:
            copy.wait()

    def arrived(sender, carry):
        @pl.when((sender != me) | (source_region != region))
        def _():
            remote(
                fc_ref.at[:, 0:window],
                ens_ref.at[pl.ds(pl.multiple_of(sender * rows, 8), rows), :],
                in_send.at[0],
                in_recv.at[sender],
                (source_region, sender),
            ).wait_recv()

        return carry

    def sent_in(w, carry):
        @pl.when(offset + w != mine)
        def _():
            in_copy(w).wait_send()

        @pl.when(offset + w == mine)
        def _():
            own_window().wait()

        return carry

    lax.fori_loop(0, count, sent_in, 0)
    lax.fori_loop(0, count, arrived, 0)

    eye_rows = lax.broadcasted_iota(jnp.int32, (members, members), 0)
    eye_columns = lax.broadcasted_iota(jnp.int32, (members, members), 1)
    identity = (eye_rows == eye_columns).astype(jnp.float32)
    tiles = tiles_ref.shape[3] // LANES
    blocks = window // BLOCK
    place = lax.broadcasted_iota(jnp.int32, (window, LANES), 0)

    flat = base * count + mine
    devices = regions * count
    near_tiles = [
        ((flat + devices - 1 + slot // tiles) % devices) * tiles + slot % tiles
        for slot in range(3 * tiles)
    ]

    def share(p, b, slot):
        listed = own_list[0, p, b : b + 1, :]
        live = lax.broadcasted_iota(jnp.int32, listed.shape, 1) < own_counts[0, p : p + 1, b : b + 1]
        hits = live & (listed == near_tiles[slot])
        return jnp.sum(hits.astype(jnp.float32), axis=1, keepdims=True)

    def exchange(p):
        state = ens_ref[...]
        high, rest = split_rest(state)
        middle, rest = split_rest(rest)
        low = rest.astype(jnp.bfloat16)
        chosen = jnp.concatenate(
            [
                (place == own_cells[0, p, t : t + 1, :]).astype(jnp.bfloat16)
                for t in range(tiles)
            ],
            axis=1,
        )

        def pick(part):
            return jnp.dot(part, chosen, preferred_element_type=jnp.float32)

        picked = pick(high) + (pick(middle) + pick(low))
        center = jnp.mean(picked, axis=0, keepdims=True)
        values = jnp.concatenate([own_values[0, p, t : t + 1, :] for t in range(tiles)], axis=1)
        weights = jnp.concatenate([own_weights[0, p, t : t + 1, :] for t in range(tiles)], axis=1)
        root_weight = jnp.sqrt(weights)
        tiles_ref[p, 1, 0:members, :] = (picked - center) * root_weight
        tiles_ref[p, 1, members : members + 8, :] = jnp.broadcast_to(
            (values - center) * root_weight, (8, values.shape[1])
        )
        copies = [
            remote(
                tiles_ref.at[p, 1], tiles_ref.at[p, 0], tile_send.at[p, 0], tile_recv.at[p, 0], nxt
            ),
            remote(
                tiles_ref.at[p, 1], tiles_ref.at[p, 2], tile_send.at[p, 1], tile_recv.at[p, 1], prv
            ),
        ]
        for copy in copies:
            copy.start()
        return copies

    def gather_systems(p, copies):
        grams = [(members - 1.0) * identity for _ in range(blocks)]
        pulls = [jnp.zeros((members, 1), jnp.float32) for _ in range(blocks)]
        for owner in (1, 0, 2):
            if owner == 0:
                for copy in copies:
                    copy.wait()
            for t in range(tiles):
                lanes = slice(t * LANES, (t + 1) * LANES)
                spread = tiles_ref[p, owner, 0:members, lanes]
                innovation = tiles_ref[p, owner, members : members + 1, lanes]
                halves = split(spread)
                gram = dot3(halves, halves, ((1,), (1,)))
                pull = jnp.sum(spread * innovation, axis=1, keepdims=True)
                slot = owner * tiles + t
                for b in range(blocks):
                    weight = share(p, b, slot)
                    grams[b] = grams[b] + weight * gram
                    pulls[b] = pulls[b] + weight * pull
        return grams, pulls

    def apply(inv_root, pull, b):
        inner = jnp.sum(inv_root * pull, axis=0, keepdims=True)
        shift = jnp.sum(inv_root * inner, axis=1, keepdims=True)
        state = ens_ref[:, b * BLOCK : (b + 1) * BLOCK]
        center = jnp.mean(state, axis=0, keepdims=True)
        anomaly = state - center
        base = center + jnp.sum(shift * anomaly, axis=0, keepdims=True)
        scaled = split(math.sqrt(members - 1) * inv_root)
        return base + dot3(scaled, split(anomaly))

    for p in range(PASSES - 1):
        grams, pulls = gather_systems(p, exchange(p))
        inv_roots = roots(grams, identity)
        for b in range(blocks):
            ens_ref[:, b * BLOCK : (b + 1) * BLOCK] = apply(inv_roots[b], pulls[b], b)

    here = pl.multiple_of(position * window, LANES)

    def out_copy(b, target):
        return remote(
            upd_ref.at[
                pl.ds(pl.multiple_of(target * rows, 8), rows), b * BLOCK : (b + 1) * BLOCK
            ],
            out_ref.at[:, pl.ds(here + b * BLOCK, BLOCK)],
            out_send.at[b, target],
            out_recv.at[b, position],
            (source_region, target),
        )

    def out_own(b):
        return pltpu.make_async_copy(
            upd_ref.at[my_rows, b * BLOCK : (b + 1) * BLOCK],
            out_ref.at[:, pl.ds(here + b * BLOCK, BLOCK)],
            local_sem.at[2 + b],
        )

    def each_target(b, remote_step, local_step):
        def go(k, carry):
            target = (me + count // 2 + k) % count
            stays = (target == me) & (source_region == region)

            @pl.when(jnp.logical_not(stays))
            def _():
                remote_step(out_copy(b, target))

            @pl.when(stays)
            def _():
                local_step(out_own(b))

            return carry

        lax.fori_loop(0, count, go, 0)

    p = PASSES - 1
    grams, pulls = gather_systems(p, exchange(p))
    for b in range(blocks):
        (inv_root,) = roots([grams[b]], identity)
        upd_ref[:, b * BLOCK : (b + 1) * BLOCK] = apply(inv_root, pulls[b], b)
        each_target(b, lambda copy: copy.start(), lambda copy: copy.start())

    for b in range(blocks):
        each_target(b, lambda copy: copy.wait_send(), lambda copy: copy.wait())

        def landed(w, carry):
            @pl.when(offset + w != mine)
            def _():
                remote(
                    upd_ref.at[0:rows, b * BLOCK : (b + 1) * BLOCK],
                    out_ref.at[
                        :, pl.ds(pl.multiple_of(w * window + b * BLOCK, LANES), BLOCK)
                    ],
                    out_send.at[b, 0],
                    out_recv.at[b, w],
                    host(offset + w),
                ).wait_recv()

            return carry

        lax.fori_loop(0, count, landed, 0)


def split_rest(value):
    high = value.astype(jnp.bfloat16)
    return high, value - high.astype(jnp.float32)


def local(
    initial_ensemble,
    driving_term,
    observation_cells,
    observation_values,
    observation_weight,
    block_tile_list,
    block_tile_count,
):
    count = lax.axis_size("member")
    regions = lax.axis_size("region")
    tiles_here = observation_cells.shape[2]
    rows, cells = initial_ensemble.shape
    members = rows * count
    window = cells // count
    blocks = window // BLOCK
    kept = pl.BlockSpec(memory_space=pl.ANY)
    wide = cells + 2 * LANES
    f32 = jnp.float32
    dma = pltpu.SemaphoreType.DMA
    return pl.pallas_call(
        functools.partial(kernel, count, regions),
        out_shape=jax.ShapeDtypeStruct((rows, cells), f32),
        in_specs=[kept] * 7,
        out_specs=kept,
        scratch_shapes=[
            pltpu.VMEM((rows, wide), f32),
            pltpu.VMEM((rows, cells), f32),
            pltpu.VMEM((members, window), f32),
            pltpu.VMEM((members, window), f32),
            pltpu.VMEM((1, wide), f32),
            pltpu.VMEM(observation_cells.shape, jnp.int32),
            pltpu.VMEM(observation_values.shape, f32),
            pltpu.VMEM(observation_weight.shape, f32),
            pltpu.VMEM(block_tile_list.shape, jnp.int32),
            pltpu.VMEM(block_tile_count.shape, jnp.int32),
            pltpu.VMEM((PASSES, 3, members + 8, tiles_here * LANES), f32),
            dma((count,)),
            dma((4,)),
            dma((4,)),
            dma((5,)),
            dma((5,)),
            dma((count,)),
            dma((count,)),
            dma((PASSES, 2)),
            dma((PASSES, 2)),
            dma((blocks, count)),
            dma((blocks, count)),
            dma((2 + blocks,)),
        ],
        compiler_params=pltpu.CompilerParams(
            collective_id=0, has_side_effects=True, vmem_limit_bytes=67_043_328
        ),
    )(
        initial_ensemble,
        driving_term[None],
        observation_cells,
        observation_values,
        observation_weight,
        block_tile_list,
        block_tile_count,
    )


def solution(mesh):
    in_specs = (
        P("member", "region"),
        P("region"),
        P(None, None, ("region", "member"), None),
        P(None, None, ("region", "member"), None),
        P(None, None, ("region", "member"), None),
        P(None, None, ("region", "member"), None),
        P(None, None, ("region", "member")),
    )
    out_specs = P("member", "region")
    return jax.shard_map(local, mesh=mesh, in_specs=in_specs, out_specs=out_specs, check_vma=False)
```

time: 93.7 us -> 86.2 us (0.920); the launches traced: 92.6 us -> 86.1 us
  Pallas kernels: 87.6 us -> 83.8 us
  other arithmetic: 1.56 us -> 0 us
  local copies, waits for them, and re-layouts: 3.48 us -> 2.26 us
    pallas_call x1, Pallas kernels: 87.6 us -> 83.8 us  [local(): pl.pallas_call(functools.partial(kernel, count, regions), out_shape=jax.S...]
    unnamed x11 -> x1, local copies, waits for them, and re-layouts: 3.48 us -> 2.26 us
where the time goes in v2:
time: 86.2 us; the launch traced here: 86.1 us
  Pallas kernels  83.8 us (97%)
  local copies, waits for them, and re-layouts  2.26 us (3%)
    pallas_call x1, Pallas kernels, local(): pl.pallas_call(functools.partial(kernel, count, regions), out_shape=jax.S...  83.8 us
    unnamed x1, local copies, waits for them, and re-layouts  2.26 us

profile of v2, /device:TPU:1, one launch (start us, length us, event | category | flops | bytes accessed | tf_op | source)
XLA Modules:
  0.0 86.1 jit_solution(8531163834176882454)
XLA Ops:
  0.0 83.8 %shard_map.73 = f32[32,8192]{1,0:T(8,128)} custom-call(f32[32,8192]{1,0:T(8,128)} %x_ref.1, f32[1,8192]{1,0:T(1,128)} %bitcast.1, s32[1,2,2,128]{3,2,1,0:T(2,128)} %cells_ref.1, f32[1,2,2,128]{3,2,1,0:T(2,128)} %values_ref.1, f32[1,2,2,128]{3,2,1,0:T(2,128)} %weights_ref.1, s32[1,2,2,4]{3,2,1,0:T(2,128)} %list_ref.1, s32[1,2,2]{2,1,0:T(2,128)} %counts_ref.1), custom_call_target="tpu_custom_call" | custom-call | tf_op jit(solution)/shard_map/pallas_call | solution.py:523
  83.8 2.3 %copy.9 = f32[32,8192]{1,0:T(8,128)} copy(f32[32,8192]{1,0:T(8,128)} %shard_map.73) | data formatting | bytes 2097152

commit v3 on v2

--- a/solution.py
+++ b/solution.py
@@ -58,7 +58,9 @@
         rts = [r + dot3(split(r), q) for r, q in zip(rts, qs)]
         return invs, rts, [close(i, r) for i, r in zip(invs, rts)]
 
-    invs, rts, errors = lax.fori_loop(0, NS_ITERS // 2 - 2, step, (invs, rts, errors))
+    invs, rts, errors = lax.fori_loop(
+        0, NS_ITERS // 2 - 2, step, (invs, rts, errors), unroll=True
+    )
     qs = [split(quartic(e)) for e in errors]
     invs = [i + dot3(split(i), q) for i, q in zip(invs, qs)]
     return [i / jnp.sqrt(f) for i, f in zip(invs, frobs)]
@@ -107,6 +109,7 @@
     own_list,
     own_counts,
     tiles_ref,
+    chosen_ref,
     load_sem,
     halo_send,
     halo_recv,
@@ -309,17 +312,42 @@
         for copy in obs_locals:
             copy.wait()
 
-    def arrived(sender, carry):
-        @pl.when((sender != me) | (source_region != region))
+    tiles = tiles_ref.shape[3] // LANES
+    place = lax.broadcasted_iota(jnp.int32, (window, LANES), 0)
+    for p in range(PASSES):
+        for t in range(tiles):
+            hit = place == own_cells[0, p, t : t + 1, :]
+            chosen_ref[p, :, t * LANES : (t + 1) * LANES] = hit.astype(jnp.bfloat16)
+
+    def pick(p, state):
+        high, rest = split_rest(state)
+        middle, rest = split_rest(rest)
+        low = rest.astype(jnp.bfloat16)
+        terms = jnp.concatenate([high, middle, low], axis=0)
+        found = jnp.dot(terms, chosen_ref[p], preferred_element_type=jnp.float32)
+        n = state.shape[0]
+        return found[:n] + (found[n : 2 * n] + found[2 * n :])
+
+    def arrived(k, carry):
+        sender = (me + k) % count
+        theirs = pl.ds(pl.multiple_of(sender * rows, 8), rows)
+        local_rows = (sender == me) & (source_region == region)
+
+        @pl.when(jnp.logical_not(local_rows))
         def _():
             remote(
                 fc_ref.at[:, 0:window],
-                ens_ref.at[pl.ds(pl.multiple_of(sender * rows, 8), rows), :],
+                ens_ref.at[theirs, :],
                 in_send.at[0],
                 in_recv.at[sender],
                 (source_region, sender),
             ).wait_recv()
 
+        @pl.when(local_rows)
+        def _():
+            own_window().wait()
+
+        tiles_ref[0, 1, theirs, :] = pick(0, ens_ref[theirs, :])
         return carry
 
     def sent_in(w, carry):
@@ -327,21 +355,14 @@
         def _():
             in_copy(w).wait_send()
 
-        @pl.when(offset + w == mine)
-        def _():
-            own_window().wait()
-
         return carry
 
-    lax.fori_loop(0, count, sent_in, 0)
     lax.fori_loop(0, count, arrived, 0)
 
     eye_rows = lax.broadcasted_iota(jnp.int32, (members, members), 0)
     eye_columns = lax.broadcasted_iota(jnp.int32, (members, members), 1)
     identity = (eye_rows == eye_columns).astype(jnp.float32)
-    tiles = tiles_ref.shape[3] // LANES
     blocks = window // BLOCK
-    place = lax.broadcasted_iota(jnp.int32, (window, LANES), 0)
 
     flat = base * count + mine
     devices = regions * count
@@ -357,22 +378,7 @@
         return jnp.sum(hits.astype(jnp.float32), axis=1, keepdims=True)
 
     def exchange(p):
-        state = ens_ref[...]
-        high, rest = split_rest(state)
-        middle, rest = split_rest(rest)
-        low = rest.astype(jnp.bfloat16)
-        chosen = jnp.concatenate(
-            [
-                (place == own_cells[0, p, t : t + 1, :]).astype(jnp.bfloat16)
-                for t in range(tiles)
-            ],
-            axis=1,
-        )
-
-        def pick(part):
-            return jnp.dot(part, chosen, preferred_element_type=jnp.float32)
-
-        picked = pick(high) + (pick(middle) + pick(low))
+        picked = pick(p, ens_ref[...]) if p else tiles_ref[0, 1, 0:members, :]
         center = jnp.mean(picked, axis=0, keepdims=True)
         values = jnp.concatenate([own_values[0, p, t : t + 1, :] for t in range(tiles)], axis=1)
         weights = jnp.concatenate([own_weights[0, p, t : t + 1, :] for t in range(tiles)], axis=1)
@@ -474,6 +480,7 @@
         upd_ref[:, b * BLOCK : (b + 1) * BLOCK] = apply(inv_root, pulls[b], b)
         each_target(b, lambda copy: copy.start(), lambda copy: copy.start())
 
+    lax.fori_loop(0, count, sent_in, 0)
     for b in range(blocks):
         each_target(b, lambda copy: copy.wait_send(), lambda copy: copy.wait())
 
@@ -537,6 +544,7 @@
             pltpu.VMEM(block_tile_list.shape, jnp.int32),
             pltpu.VMEM(block_tile_count.shape, jnp.int32),
             pltpu.VMEM((PASSES, 3, members + 8, tiles_here * LANES), f32),
+            pltpu.VMEM((PASSES, window, tiles_here * LANES), jnp.bfloat16),
             dma((count,)),
             dma((4,)),
             dma((4,)),

time: 86.2 us -> 83.9 us (0.973)
  Pallas kernels: 83.8 us -> 81.5 us
    pallas_call x1, Pallas kernels: 83.8 us -> 81.5 us  [local(): pl.pallas_call(functools.partial(kernel, count, regions), out_shape=jax.S...]
where the time goes in v3:
time: 83.9 us; the launch traced here: 83.8 us
  Pallas kernels  81.5 us (97%)
  local copies, waits for them, and re-layouts  2.26 us (3%)
    pallas_call x1, Pallas kernels, local(): pl.pallas_call(functools.partial(kernel, count, regions), out_shape=jax.S...  81.5 us
    unnamed x1, local copies, waits for them, and re-layouts  2.26 us

profile of v3, /device:TPU:1, one launch (start us, length us, event | category | flops | bytes accessed | tf_op | source)
XLA Modules:
  0.0 83.8 jit_solution(15028325704217776887)
XLA Ops:
  0.0 81.5 %shard_map.73 = f32[32,8192]{1,0:T(8,128)} custom-call(f32[32,8192]{1,0:T(8,128)} %x_ref.1, f32[1,8192]{1,0:T(1,128)} %bitcast.1, s32[1,2,2,128]{3,2,1,0:T(2,128)} %cells_ref.1, f32[1,2,2,128]{3,2,1,0:T(2,128)} %values_ref.1, f32[1,2,2,128]{3,2,1,0:T(2,128)} %weights_ref.1, s32[1,2,2,4]{3,2,1,0:T(2,128)} %list_ref.1, s32[1,2,2]{2,1,0:T(2,128)} %counts_ref.1), custom_call_target="tpu_custom_call" | custom-call | tf_op jit(solution)/shard_map/pallas_call | solution.py:530
  81.5 2.3 %copy.9 = f32[32,8192]{1,0:T(8,128)} copy(f32[32,8192]{1,0:T(8,128)} %shard_map.73) | data formatting | bytes 2097152

commit v4 on v3

--- a/solution.py
+++ b/solution.py
@@ -32,7 +32,7 @@
 
 def roots(systems, identity):
     frobs = [jnp.sqrt(jnp.sum(s * s, keepdims=True)) for s in systems]
-    firsts = [s / f for s, f in zip(systems, frobs)]
+    firsts = [s * (1.0 / f) for s, f in zip(systems, frobs)]
 
     def quartic(error):
         halves = split(error)
@@ -63,7 +63,7 @@
     )
     qs = [split(quartic(e)) for e in errors]
     invs = [i + dot3(split(i), q) for i, q in zip(invs, qs)]
-    return [i / jnp.sqrt(f) for i, f in zip(invs, frobs)]
+    return [i * (1.0 / jnp.sqrt(f)) for i, f in zip(invs, frobs)]
 
 
 def snake_member(position, count):
@@ -403,9 +403,8 @@
         grams = [(members - 1.0) * identity for _ in range(blocks)]
         pulls = [jnp.zeros((members, 1), jnp.float32) for _ in range(blocks)]
         for owner in (1, 0, 2):
-            if owner == 0:
-                for copy in copies:
-                    copy.wait()
+            if owner != 1:
+                copies[owner // 2].wait()
             for t in range(tiles):
                 lanes = slice(t * LANES, (t + 1) * LANES)
                 spread = tiles_ref[p, owner, 0:members, lanes]

time: 83.9 us -> 83.7 us (level)
  no operation moved by 1% of the time
where the time goes in v4:
time: 83.7 us; the launch traced here: 83.6 us
  Pallas kernels  81.3 us (97%)
  local copies, waits for them, and re-layouts  2.26 us (3%)
    pallas_call x1, Pallas kernels, local(): pl.pallas_call(functools.partial(kernel, count, regions), out_shape=jax.S...  81.3 us
    unnamed x1, local copies, waits for them, and re-layouts  2.26 us

profile of v4, /device:TPU:1, one launch (start us, length us, event | category | flops | bytes accessed | tf_op | source)
XLA Modules:
  0.0 83.6 jit_solution(5982184696342798776)
XLA Ops:
  0.0 81.3 %shard_map.73 = f32[32,8192]{1,0:T(8,128)} custom-call(f32[32,8192]{1,0:T(8,128)} %x_ref.1, f32[1,8192]{1,0:T(1,128)} %bitcast.1, s32[1,2,2,128]{3,2,1,0:T(2,128)} %cells_ref.1, f32[1,2,2,128]{3,2,1,0:T(2,128)} %values_ref.1, f32[1,2,2,128]{3,2,1,0:T(2,128)} %weights_ref.1, s32[1,2,2,4]{3,2,1,0:T(2,128)} %list_ref.1, s32[1,2,2]{2,1,0:T(2,128)} %counts_ref.1), custom_call_target="tpu_custom_call" | custom-call | tf_op jit(solution)/shard_map/pallas_call | solution.py:529
  81.3 2.3 %copy.9 = f32[32,8192]{1,0:T(8,128)} copy(f32[32,8192]{1,0:T(8,128)} %shard_map.73) | data formatting | bytes 2097152
